TPU v7x, 32 devices: a whole 2x2x4 slice. The times are simulated.
32 devices in a mesh: rep: 8 (over z, x), rows: 4 (over y, core).
Axes of the slice: x: 2, y: 2, z: 4, core: 2. Of those that a mesh axis runs over, the one named last changes fastest.
Arguments:
- pooled_grad: bfloat16 [32768, 2, 128], P(('rep', 'rows')), may hold values from -6 to 6
- slot_source: int32 [32, 4, 1024], P(('rep', 'rows')), may hold values from 0 to 2047, as said below
- slot_target: int32 [32, 4, 1024], P(('rep', 'rows')), may hold values from 0 to 8191, as said below
- slot_count: int32 [32, 4], P(('rep', 'rows')), may hold values from 128 to 1024, as said below
- table_rows: float32 [2, 16384, 128], P(None, 'rows'), may hold values from -1.5 to 1.5
- accum: float32 [2, 16384], P(None, 'rows'), may hold values from 0.01 to 1
Outputs:
- new_rows: float32 [2, 16384, 128], P(None, 'rows')
- new_accum: float32 [2, 16384], P(None, 'rows')
Inputs may be any that keep to these rules, and one draw needn't show every extreme that they name: `slot_source`: entry q encodes a local sample q // 2 and a table q % 2; the table agrees with that of slot_target at the same slot. `slot_target`: entry t encodes a table t // 4096 and a row t % 4096 of the owner's shard; rows repeat across slots and senders. `slot_count`: slots at or past the count carry no lookup; every sender fills all slots to some owner.
All inputs are finite; a program needn't handle non-finite values.
Results may differ from a plain program's by a relative error of at most 0.0003.
Values may be sent and summed in bfloat16 or wider, within the bound.
A program may use at most 64 MiB of HBM per device.

v0:
```python
import math
import jax
import jax.numpy as jnp
from jax import lax
from jax.sharding import PartitionSpec as P

LEARN_RATE = 0.1
EPSILON = 1e-06


def accumulate(grads, targets, tables, rows_dev):
    feature = grads.shape[-1]
    flat_rows = grads.reshape(-1, feature)
    lookup_keys = targets.reshape(-1)
    row_total = tables * rows_dev
    block_size = math.gcd(row_total, 512)
    block_count = row_total // block_size
    offsets = jnp.arange(block_size, dtype=jnp.int32)

    def row_block(block_index):
        row_base = block_index * block_size
        matches = (lookup_keys[:, None] == row_base + offsets[None, :]).astype(jnp.bfloat16)
        return jnp.einsum("sr,sw->rw", matches, flat_rows, preferred_element_type=jnp.float32)

    blocks = lax.map(row_block, jnp.arange(block_count, dtype=jnp.int32))
    return blocks.reshape(tables, rows_dev, feature)


def pick_rows(flat_grad, lookup_keys):
    slot_total = lookup_keys.shape[0]
    block_size = math.gcd(slot_total, 1024)
    block_count = slot_total // block_size
    sources = jnp.arange(flat_grad.shape[0], dtype=jnp.int32)
    key_blocks = lookup_keys.reshape(block_count, block_size)

    def slot_block(block_keys):
        matches = (block_keys[:, None] == sources[None, :]).astype(jnp.bfloat16)
        return jnp.dot(matches, flat_grad, preferred_element_type=jnp.float32).astype(jnp.bfloat16)

    blocks = lax.map(slot_block, key_blocks)
    return blocks.reshape(slot_total, flat_grad.shape[1])


def adagrad(rows_part, state_part, row_grad):
    updated = state_part + jnp.mean(row_grad * row_grad, axis=2)
    shifted = rows_part - LEARN_RATE * row_grad / (jnp.sqrt(updated)[:, :, None] + EPSILON)
    return (shifted, updated)


def shards(pooled_grad, slot_source, slot_target, slot_count, table_rows, accum):
    tables = pooled_grad.shape[1]
    feature = pooled_grad.shape[2]
    rows_dev = table_rows.shape[1]
    owner_total = slot_source.shape[1]
    slot_total = slot_source.shape[2]
    flat_grad = pooled_grad.reshape(-1, feature)
    source = slot_source[0]
    target = slot_target[0]
    counts = slot_count[0]
    slot_ids = jnp.arange(slot_total, dtype=jnp.int32)
    filled = slot_ids[None, :] < counts[:, None]
    source_keys = jnp.where(filled, source, -1).reshape(-1)
    picked = pick_rows(flat_grad, source_keys).reshape(owner_total, slot_total, feature)
    targets = jnp.where(filled, target, -1)
    got_grads, got_targets = (
        lax.all_to_all(picked, "rows", split_axis=0, concat_axis=0, tiled=True),
        lax.all_to_all(targets, "rows", split_axis=0, concat_axis=0, tiled=True),
    )
    partial_grad = accumulate(got_grads, got_targets, tables, rows_dev)
    row_grad = lax.psum(partial_grad, "rep")
    new_rows, new_accum = adagrad(table_rows, accum, row_grad)
    return (new_rows, new_accum)


def solution(mesh):
    in_specs = (
        P(("rep", "rows"), None, None),
        P(("rep", "rows"), None, None),
        P(("rep", "rows"), None, None),
        P(("rep", "rows"), None),
        P(None, "rows", None),
        P(None, "rows"),
    )
    out_specs = (P(None, "rows", None), P(None, "rows"))
    return jax.shard_map(shards, mesh=mesh, in_specs=in_specs, out_specs=out_specs, check_vma=False)
```

profile of v0, /device:TPU:0, one launch (start us, length us, event | category | flops | bytes accessed | tf_op | source)
XLA Modules:
  0.0 295.6 jit_solution(14990334803559282214)
XLA Ops:
  7.2 1.4 compare_select_fusion
  8.6 4.3 %all-to-all-start = ((s32[4,1,1024]{2,1,0:T(1,128)}), s32[4,1,1024]{2,1,0:T(1,128)S(1)}, u32[]{:S(2)}, u32[]{:S(2)}) async-start(s32[4,1,1024]{2,1,0:T(1,128)} %compare_select_fusion), calls=%async_computation | async-start | bytes 32768 | tf_op jit(solution)/shard_map/all_to_all | solution.py:67
  12.8 0.8 bitcast_select_fusion
  13.6 12.9 %while.22 = (s32[]{:T(128)}, bf16[4,1024,128]{2,1,0:T(8,128)(2,1)}, s32[4,1024]{1,0:T(4,128)S(1)}, bf16[2048,128]{1,0:T(8,128)(2,1)}, s32[]{:T(128)}) while((s32[]{:T(128)}, bf16[4,1024,128]{2,1,0:T(8,128)(2,1)}, s32[4,1024]{1,0:T(4,128)S(1)}, bf16[2048,128]{1,0:T(8,128)(2,1)}, s32[]{:T(128)}) %tuple.52), condition=%wide.region_1.2_spmd.clone, body=%wide.region_0.1_spmd.clone.sunk | while | flops 539099136 | bytes 799297 | solution.py:40
  13.6 3.2 %fusion.27 = bf16[4,1024,128]{2,1,0:T(8,128)(2,1)} fusion(bf16[4,1024,128]{2,1,0:T(8,128)(2,1)} %get-tuple-element.167, s32[]{:T(128)} %get-tuple-element.166, bf16[2048,128]{1,0:T(8,128)(2,1)} %get-tuple-element.174, s32[1024]{0:T(1024)S(1)} %bitcast.46), kind=kOutput, calls=%fused_computation.7.clone.1 | convolution fusion | flops 539099136 | bytes 791040 | tf_op jit(solution)/shard_map/while/body/eval_jaxpr/dot_general | solution.py:38
  16.9 3.2 %fusion.27 = bf16[4,1024,128]{2,1,0:T(8,128)(2,1)} fusion(bf16[4,1024,128]{2,1,0:T(8,128)(2,1)} %get-tuple-element.167, s32[]{:T(128)} %get-tuple-element.166, bf16[2048,128]{1,0:T(8,128)(2,1)} %get-tuple-element.174, s32[1024]{0:T(1024)S(1)} %bitcast.46), kind=kOutput, calls=%fused_computation.7.clone.1 | convolution fusion | flops 539099136 | bytes 791040 | tf_op jit(solution)/shard_map/while/body/eval_jaxpr/dot_general | solution.py:38
  20.1 3.2 %fusion.27 = bf16[4,1024,128]{2,1,0:T(8,128)(2,1)} fusion(bf16[4,1024,128]{2,1,0:T(8,128)(2,1)} %get-tuple-element.167, s32[]{:T(128)} %get-tuple-element.166, bf16[2048,128]{1,0:T(8,128)(2,1)} %get-tuple-element.174, s32[1024]{0:T(1024)S(1)} %bitcast.46), kind=kOutput, calls=%fused_computation.7.clone.1 | convolution fusion | flops 539099136 | bytes 791040 | tf_op jit(solution)/shard_map/while/body/eval_jaxpr/dot_general | solution.py:38
  23.3 3.2 %fusion.27 = bf16[4,1024,128]{2,1,0:T(8,128)(2,1)} fusion(bf16[4,1024,128]{2,1,0:T(8,128)(2,1)} %get-tuple-element.167, s32[]{:T(128)} %get-tuple-element.166, bf16[2048,128]{1,0:T(8,128)(2,1)} %get-tuple-element.174, s32[1024]{0:T(1024)S(1)} %bitcast.46), kind=kOutput, calls=%fused_computation.7.clone.1 | convolution fusion | flops 539099136 | bytes 791040 | tf_op jit(solution)/shard_map/while/body/eval_jaxpr/dot_general | solution.py:38
  26.6 3.5 %all-to-all-start.1 = ((bf16[4,1024,128]{2,1,0:T(8,128)(2,1)}), bf16[4,1024,128]{2,1,0:T(8,128)(2,1)S(1)}, u32[]{:S(2)}, u32[]{:S(2)}) async-start(bf16[4,1024,128]{2,1,0:T(8,128)(2,1)} %get-tuple-element.61), calls=%async_computation.1 | async-start | bytes 2097152 | tf_op jit(solution)/shard_map/all_to_all | solution.py:66
  30.2 14.3 %all-to-all-done.1 = bf16[4,1024,128]{2,1,0:T(8,128)(2,1)S(1)} async-done(((bf16[4,1024,128]{2,1,0:T(8,128)(2,1)}), bf16[4,1024,128]{2,1,0:T(8,128)(2,1)S(1)}, u32[]{:S(2)}, u32[]{:S(2)}) %all-to-all-start.1) | async-done | bytes 1048608 | tf_op jit(solution)/shard_map/all_to_all | solution.py:66
  44.5 78.5 %while.23 = (s32[]{:T(128)}, f32[16,512,128]{2,1,0:T(8,128)}, s32[4,1024]{1,0:T(4,128)S(1)}, s32[16]{0:T(128)S(1)}, bf16[4096,128]{1,0:T(8,128)(2,1)S(1)}, /*index=5*/s32[]{:T(128)}, s32[1]{0:T(128)}) while((s32[]{:T(128)}, f32[16,512,128]{2,1,0:T(8,128)}, s32[4,1024]{1,0:T(4,128)S(1)}, s32[16]{0:T(128)S(1)}, ...), condition=%wide.region_3.4_spmd.clone, body=%wide.region_2.3_spmd.clone.sunk | while | flops 538968576 | bytes 1364585 | solution.py:25
  44.5 0.6 dynamic_slice.14
  45.7 3.7 %fusion.30 = f32[16,512,128]{2,1,0:T(8,128)} fusion(f32[16,512,128]{2,1,0:T(8,128)} %get-tuple-element.184, s32[]{:T(128)} %get-tuple-element.183, bf16[4096,128]{1,0:T(8,128)(2,1)S(1)} %get-tuple-element.194, s32[512]{0:T(512)S(1)} %iota_add_fusion.2, s32[4096]{0:T(1024)S(1)} %bitcast.45), kind=kOutput, calls=%fused_computation.14.clone.1 | convolution fusion | flops 538968064 | bytes 1329664 | tf_op jit(solution)/shard_map/while/body/eval_jaxpr/sr,sw->rw/dot_general | solution.py:23
  50.7 3.7 %fusion.30 = f32[16,512,128]{2,1,0:T(8,128)} fusion(f32[16,512,128]{2,1,0:T(8,128)} %get-tuple-element.184, s32[]{:T(128)} %get-tuple-element.183, bf16[4096,128]{1,0:T(8,128)(2,1)S(1)} %get-tuple-element.194, s32[512]{0:T(512)S(1)} %iota_add_fusion.2, s32[4096]{0:T(1024)S(1)} %bitcast.45), kind=kOutput, calls=%fused_computation.14.clone.1 | convolution fusion | flops 538968064 | bytes 1329664 | tf_op jit(solution)/shard_map/while/body/eval_jaxpr/sr,sw->rw/dot_general | solution.py:23
  55.6 3.7 %fusion.30 = f32[16,512,128]{2,1,0:T(8,128)} fusion(f32[16,512,128]{2,1,0:T(8,128)} %get-tuple-element.184, s32[]{:T(128)} %get-tuple-element.183, bf16[4096,128]{1,0:T(8,128)(2,1)S(1)} %get-tuple-element.194, s32[512]{0:T(512)S(1)} %iota_add_fusion.2, s32[4096]{0:T(1024)S(1)} %bitcast.45), kind=kOutput, calls=%fused_computation.14.clone.1 | convolution fusion | flops 538968064 | bytes 1329664 | tf_op jit(solution)/shard_map/while/body/eval_jaxpr/sr,sw->rw/dot_general | solution.py:23
  60.5 3.7 %fusion.30 = f32[16,512,128]{2,1,0:T(8,128)} fusion(f32[16,512,128]{2,1,0:T(8,128)} %get-tuple-element.184, s32[]{:T(128)} %get-tuple-element.183, bf16[4096,128]{1,0:T(8,128)(2,1)S(1)} %get-tuple-element.194, s32[512]{0:T(512)S(1)} %iota_add_fusion.2, s32[4096]{0:T(1024)S(1)} %bitcast.45), kind=kOutput, calls=%fused_computation.14.clone.1 | convolution fusion | flops 538968064 | bytes 1329664 | tf_op jit(solution)/shard_map/while/body/eval_jaxpr/sr,sw->rw/dot_general | solution.py:23
  65.4 3.7 %fusion.30 = f32[16,512,128]{2,1,0:T(8,128)} fusion(f32[16,512,128]{2,1,0:T(8,128)} %get-tuple-element.184, s32[]{:T(128)} %get-tuple-element.183, bf16[4096,128]{1,0:T(8,128)(2,1)S(1)} %get-tuple-element.194, s32[512]{0:T(512)S(1)} %iota_add_fusion.2, s32[4096]{0:T(1024)S(1)} %bitcast.45), kind=kOutput, calls=%fused_computation.14.clone.1 | convolution fusion | flops 538968064 | bytes 1329664 | tf_op jit(solution)/shard_map/while/body/eval_jaxpr/sr,sw->rw/dot_general | solution.py:23
  70.3 3.7 %fusion.30 = f32[16,512,128]{2,1,0:T(8,128)} fusion(f32[16,512,128]{2,1,0:T(8,128)} %get-tuple-element.184, s32[]{:T(128)} %get-tuple-element.183, bf16[4096,128]{1,0:T(8,128)(2,1)S(1)} %get-tuple-element.194, s32[512]{0:T(512)S(1)} %iota_add_fusion.2, s32[4096]{0:T(1024)S(1)} %bitcast.45), kind=kOutput, calls=%fused_computation.14.clone.1 | convolution fusion | flops 538968064 | bytes 1329664 | tf_op jit(solution)/shard_map/while/body/eval_jaxpr/sr,sw->rw/dot_general | solution.py:23
  75.2 3.7 %fusion.30 = f32[16,512,128]{2,1,0:T(8,128)} fusion(f32[16,512,128]{2,1,0:T(8,128)} %get-tuple-element.184, s32[]{:T(128)} %get-tuple-element.183, bf16[4096,128]{1,0:T(8,128)(2,1)S(1)} %get-tuple-element.194, s32[512]{0:T(512)S(1)} %iota_add_fusion.2, s32[4096]{0:T(1024)S(1)} %bitcast.45), kind=kOutput, calls=%fused_computation.14.clone.1 | convolution fusion | flops 538968064 | bytes 1329664 | tf_op jit(solution)/shard_map/while/body/eval_jaxpr/sr,sw->rw/dot_general | solution.py:23
  80.1 3.7 %fusion.30 = f32[16,512,128]{2,1,0:T(8,128)} fusion(f32[16,512,128]{2,1,0:T(8,128)} %get-tuple-element.184, s32[]{:T(128)} %get-tuple-element.183, bf16[4096,128]{1,0:T(8,128)(2,1)S(1)} %get-tuple-element.194, s32[512]{0:T(512)S(1)} %iota_add_fusion.2, s32[4096]{0:T(1024)S(1)} %bitcast.45), kind=kOutput, calls=%fused_computation.14.clone.1 | convolution fusion | flops 538968064 | bytes 1329664 | tf_op jit(solution)/shard_map/while/body/eval_jaxpr/sr,sw->rw/dot_general | solution.py:23
  85.0 3.7 %fusion.30 = f32[16,512,128]{2,1,0:T(8,128)} fusion(f32[16,512,128]{2,1,0:T(8,128)} %get-tuple-element.184, s32[]{:T(128)} %get-tuple-element.183, bf16[4096,128]{1,0:T(8,128)(2,1)S(1)} %get-tuple-element.194, s32[512]{0:T(512)S(1)} %iota_add_fusion.2, s32[4096]{0:T(1024)S(1)} %bitcast.45), kind=kOutput, calls=%fused_computation.14.clone.1 | convolution fusion | flops 538968064 | bytes 1329664 | tf_op jit(solution)/shard_map/while/body/eval_jaxpr/sr,sw->rw/dot_general | solution.py:23
  89.9 3.7 %fusion.30 = f32[16,512,128]{2,1,0:T(8,128)} fusion(f32[16,512,128]{2,1,0:T(8,128)} %get-tuple-element.184, s32[]{:T(128)} %get-tuple-element.183, bf16[4096,128]{1,0:T(8,128)(2,1)S(1)} %get-tuple-element.194, s32[512]{0:T(512)S(1)} %iota_add_fusion.2, s32[4096]{0:T(1024)S(1)} %bitcast.45), kind=kOutput, calls=%fused_computation.14.clone.1 | convolution fusion | flops 538968064 | bytes 1329664 | tf_op jit(solution)/shard_map/while/body/eval_jaxpr/sr,sw->rw/dot_general | solution.py:23
  94.8 3.7 %fusion.30 = f32[16,512,128]{2,1,0:T(8,128)} fusion(f32[16,512,128]{2,1,0:T(8,128)} %get-tuple-element.184, s32[]{:T(128)} %get-tuple-element.183, bf16[4096,128]{1,0:T(8,128)(2,1)S(1)} %get-tuple-element.194, s32[512]{0:T(512)S(1)} %iota_add_fusion.2, s32[4096]{0:T(1024)S(1)} %bitcast.45), kind=kOutput, calls=%fused_computation.14.clone.1 | convolution fusion | flops 538968064 | bytes 1329664 | tf_op jit(solution)/shard_map/while/body/eval_jaxpr/sr,sw->rw/dot_general | solution.py:23
  99.7 3.7 %fusion.30 = f32[16,512,128]{2,1,0:T(8,128)} fusion(f32[16,512,128]{2,1,0:T(8,128)} %get-tuple-element.184, s32[]{:T(128)} %get-tuple-element.183, bf16[4096,128]{1,0:T(8,128)(2,1)S(1)} %get-tuple-element.194, s32[512]{0:T(512)S(1)} %iota_add_fusion.2, s32[4096]{0:T(1024)S(1)} %bitcast.45), kind=kOutput, calls=%fused_computation.14.clone.1 | convolution fusion | flops 538968064 | bytes 1329664 | tf_op jit(solution)/shard_map/while/body/eval_jaxpr/sr,sw->rw/dot_general | solution.py:23
  104.6 3.7 %fusion.30 = f32[16,512,128]{2,1,0:T(8,128)} fusion(f32[16,512,128]{2,1,0:T(8,128)} %get-tuple-element.184, s32[]{:T(128)} %get-tuple-element.183, bf16[4096,128]{1,0:T(8,128)(2,1)S(1)} %get-tuple-element.194, s32[512]{0:T(512)S(1)} %iota_add_fusion.2, s32[4096]{0:T(1024)S(1)} %bitcast.45), kind=kOutput, calls=%fused_computation.14.clone.1 | convolution fusion | flops 538968064 | bytes 1329664 | tf_op jit(solution)/shard_map/while/body/eval_jaxpr/sr,sw->rw/dot_general | solution.py:23
  109.6 3.7 %fusion.30 = f32[16,512,128]{2,1,0:T(8,128)} fusion(f32[16,512,128]{2,1,0:T(8,128)} %get-tuple-element.184, s32[]{:T(128)} %get-tuple-element.183, bf16[4096,128]{1,0:T(8,128)(2,1)S(1)} %get-tuple-element.194, s32[512]{0:T(512)S(1)} %iota_add_fusion.2, s32[4096]{0:T(1024)S(1)} %bitcast.45), kind=kOutput, calls=%fused_computation.14.clone.1 | convolution fusion | flops 538968064 | bytes 1329664 | tf_op jit(solution)/shard_map/while/body/eval_jaxpr/sr,sw->rw/dot_general | solution.py:23
  114.5 3.7 %fusion.30 = f32[16,512,128]{2,1,0:T(8,128)} fusion(f32[16,512,128]{2,1,0:T(8,128)} %get-tuple-element.184, s32[]{:T(128)} %get-tuple-element.183, bf16[4096,128]{1,0:T(8,128)(2,1)S(1)} %get-tuple-element.194, s32[512]{0:T(512)S(1)} %iota_add_fusion.2, s32[4096]{0:T(1024)S(1)} %bitcast.45), kind=kOutput, calls=%fused_computation.14.clone.1 | convolution fusion | flops 538968064 | bytes 1329664 | tf_op jit(solution)/shard_map/while/body/eval_jaxpr/sr,sw->rw/dot_general | solution.py:23
  119.4 3.7 %fusion.30 = f32[16,512,128]{2,1,0:T(8,128)} fusion(f32[16,512,128]{2,1,0:T(8,128)} %get-tuple-element.184, s32[]{:T(128)} %get-tuple-element.183, bf16[4096,128]{1,0:T(8,128)(2,1)S(1)} %get-tuple-element.194, s32[512]{0:T(512)S(1)} %iota_add_fusion.2, s32[4096]{0:T(1024)S(1)} %bitcast.45), kind=kOutput, calls=%fused_computation.14.clone.1 | convolution fusion | flops 538968064 | bytes 1329664 | tf_op jit(solution)/shard_map/while/body/eval_jaxpr/sr,sw->rw/dot_general | solution.py:23
  123.0 157.3 %all-reduce.2.cloned.1.call-done = f32[2,4096,128]{2,1,0:T(8,128)} async-done(((f32[2,4096,128]{2,1,0:T(8,128)}), f32[2,4096,128]{2,1,0:T(8,128)}) %all-reduce.2.cloned.1.call-update) | async-done | bytes 4194320 | tf_op jit(solution)/shard_map/psum | solution.py:70
  280.4 3.5 %multiply_reduce_fusion = f32[2,4096]{1,0:T(2,128)S(1)} fusion(f32[2,4096,128]{2,1,0:T(8,128)} %all-reduce.2.cloned.1.call-done), kind=kLoop, calls=%fused_computation.18 | loop fusion | flops 2088960 | bytes 4227072 | tf_op jit(solution)/shard_map/reduce_sum | solution.py:45
  283.9 0.7 sqrt_add_fusion
  284.6 4.2 %divide_subtract_fusion = f32[2,4096,128]{2,1,0:T(8,128)} fusion(f32[2,4096,128]{2,1,0:T(8,128)} %param.14, f32[2,4096,128]{2,1,0:T(8,128)S(1)} %copy-done, f32[2,4096]{1,0:T(2,128)S(1)} %get-tuple-element.103), kind=kLoop, calls=%fused_computation.17 | loop fusion | flops 3145728 | bytes 12615680 | tf_op jit(solution)/shard_map/sub | solution.py:46
  (62 shorter events, 8.9 us)
Async XLA Ops:
  8.6 18.0 %all-to-all-start = ((s32[4,1,1024]{2,1,0:T(1,128)}), s32[4,1,1024]{2,1,0:T(1,128)S(1)}, u32[]{:S(2)}, u32[]{:S(2)}) async-start(s32[4,1,1024]{2,1,0:T(1,128)} %compare_select_fusion), calls=%async_computation | async-start | bytes 32768 | tf_op jit(solution)/shard_map/all_to_all | solution.py:67
  26.6 17.9 %all-to-all-start.1 = ((bf16[4,1024,128]{2,1,0:T(8,128)(2,1)}), bf16[4,1024,128]{2,1,0:T(8,128)(2,1)S(1)}, u32[]{:S(2)}, u32[]{:S(2)}) async-start(bf16[4,1024,128]{2,1,0:T(8,128)(2,1)} %get-tuple-element.61), calls=%async_computation.1 | async-start | bytes 2097152 | tf_op jit(solution)/shard_map/all_to_all | solution.py:66
  30.1 250.3 %all-reduce.2.cloned.1.call-start = ((), (), s32[]{:S(2)}) async-start(), calls=%async_computation.2 | async-start | bytes 8388608 | tf_op jit(solution)/shard_map/psum | solution.py:70
  123.0 160.9 %copy-start.1 = (f32[2,4096]{1,0:T(2,128)S(1)}, f32[2,4096]{1,0:T(2,128)}, u32[]{:S(2)}) copy-start(f32[2,4096]{1,0:T(2,128)} %param.15) | copy-start | bytes 98308
  280.4 4.2 %copy-start = (f32[2,4096,128]{2,1,0:T(8,128)S(1)}, f32[2,4096,128]{2,1,0:T(8,128)}, u32[]{:S(2)}) copy-start(f32[2,4096,128]{2,1,0:T(8,128)} %all-reduce.2.cloned.1.call-done) | copy-start | bytes 12582916
Sparse Core Ops, SparseCore 0:
  123.2 157.1 all-reduce.1
where the time goes:
time: 296 us
  waiting for transfers between devices  172 us (58%)
  matrix products  71.3 us (24%)
  between operations  14.1 us (5%)
  loops' own time  10.7 us (4%)
  other arithmetic  10.6 us (4%)
  local copies, waits for them, and re-layouts  9.41 us (3%)
  starting transfers between devices  7.82 us (3%)
    psum x1, waiting for transfers between devices, shards(): row_grad = lax.psum(partial_grad, 'rep')  157 us
    dot_general x16, matrix products, row_block(): jnp.einsum('sr,sw->rw', matches, flat_rows, preferred_element_type=jnp.fl...  58.4 us
    all_to_all x1, waiting for transfers between devices, shards(): lax.all_to_all(picked, 'rows', split_axis=0, concat_axis=0, tiled=True)  14.3 us
    dot_general x4, matrix products, slot_block(): jnp.dot(matches, flat_grad, preferred_element_type=jnp.float32)  12.9 us
    another operation x1, loops' own time, accumulate(): blocks = lax.map(row_block, jnp.arange(block_count, dtype=jnp.int32))  10.7 us
    dynamic_slice x16, local copies, waits for them, and re-layouts, accumulate(): blocks = lax.map(row_block, jnp.arange(block_count, dtype=jnp.int32))  9.32 us
  transfers between devices with their start and end apart: 3, of which 2 were waited for; matrix products, arithmetic and copies ran while one was open for 5% of the time, Pallas kernels for 0%

commit v1 on v0

--- a/solution.py
+++ b/solution.py
@@ -67,7 +67,24 @@
         lax.all_to_all(targets, "rows", split_axis=0, concat_axis=0, tiled=True),
     )
     partial_grad = accumulate(got_grads, got_targets, tables, rows_dev)
-    row_grad = lax.psum(partial_grad, "rep")
+
+    def inputs_treat(packet):
+        lane_axis = "rep"
+        k_all = jax.lax.axis_size(lane_axis)
+
+        def run_sector(o_now, w_next):
+            if w_next >= k_all:
+                return o_now
+            far_arr = run_sector(
+                o_now + jax.lax.ppermute(o_now, lane_axis, [(q, q ^ w_next) for q in range(k_all)]),
+                2 * w_next,
+            )
+            return far_arr
+
+        q_next = run_sector(packet, 1)
+        return q_next
+
+    row_grad = inputs_treat(partial_grad)
     new_rows, new_accum = adagrad(table_rows, accum, row_grad)
     return (new_rows, new_accum)
 

time: 296 us -> 491 us (1.66)
  waiting for transfers between devices: 172 us -> 373 us
  between operations: 14.1 us -> 0.69 us
  starting transfers between devices: 7.82 us -> 14.3 us
    ppermute x0 -> x3, waiting for transfers between devices: none -> 359 us  [run_sector(): jax.lax.ppermute(o_now, lane_axis, [(q, q ^ w_next) for q in range(k_all)])]
    psum x1 -> x0, waiting for transfers between devices: 157 us -> none  [shards(): row_grad = lax.psum(partial_grad, 'rep')]
    ppermute x0 -> x3, starting transfers between devices: none -> 6.55 us  [run_sector(): jax.lax.ppermute(o_now, lane_axis, [(q, q ^ w_next) for q in range(k_all)])]
  transfers between devices with their start and end apart: 3 -> 5, of which waited for: 2 -> 4; matrix products, arithmetic and copies ran while one was open for 5% -> 3% of each run, Pallas kernels for 0% -> 0%
where the time goes in v1:
time: 491 us; the launch traced here: 490 us
  waiting for transfers between devices  373 us (76%)
  matrix products  71.3 us (15%)
  starting transfers between devices  14.3 us (3%)
  loops' own time  10.7 us (2%)
  other arithmetic  10.4 us (2%)
  local copies, waits for them, and re-layouts  9.42 us (2%)
    ppermute x3, waiting for transfers between devices, run_sector(): jax.lax.ppermute(o_now, lane_axis, [(q, q ^ w_next) for q in range(k_all)])  359 us
    dot_general x16, matrix products, row_block(): jnp.einsum('sr,sw->rw', matches, flat_rows, preferred_element_type=jnp.fl...  58.4 us
    all_to_all x1, waiting for transfers between devices, shards(): lax.all_to_all(picked, 'rows', split_axis=0, concat_axis=0, tiled=True)  14.4 us
    dot_general x4, matrix products, slot_block(): jnp.dot(matches, flat_grad, preferred_element_type=jnp.float32)  12.9 us
    another operation x1, loops' own time, accumulate(): blocks = lax.map(row_block, jnp.arange(block_count, dtype=jnp.int32))  10.7 us
  transfers between devices with their start and end apart: 5, of which 4 were waited for; matrix products, arithmetic and copies ran while one was open for 3% of the time, Pallas kernels for 0%

profile of v1, /device:TPU:0, one launch (start us, length us, event | category | flops | bytes accessed | tf_op | source)
XLA Modules:
  0.0 490.0 jit_solution(15269057772257923536)
XLA Ops:
  2.0 4.3 all-to-all-start
  7.1 12.9 %while.22 = (s32[]{:T(128)}, bf16[4,1024,128]{2,1,0:T(8,128)(2,1)}, s32[4,1024]{1,0:T(4,128)S(1)}, bf16[2048,128]{1,0:T(8,128)(2,1)}, s32[]{:T(128)}) while((s32[]{:T(128)}, bf16[4,1024,128]{2,1,0:T(8,128)(2,1)}, s32[4,1024]{1,0:T(4,128)S(1)}, bf16[2048,128]{1,0:T(8,128)(2,1)}, s32[]{:T(128)}) %tuple.50), condition=%wide.region_1.2_spmd.clone, body=%wide.region_0.1_spmd.clone.sunk | while | flops 539099136 | bytes 798797 | solution.py:40
  7.1 3.2 fusion.27
  10.3 3.2 fusion.27
  13.6 3.2 fusion.27
  16.8 3.2 fusion.27
  20.0 3.5 all-to-all-start.1
  23.6 14.4 %all-to-all-done.1 = bf16[4,1024,128]{2,1,0:T(8,128)(2,1)S(1)} async-done(((bf16[4,1024,128]{2,1,0:T(8,128)(2,1)}), bf16[4,1024,128]{2,1,0:T(8,128)(2,1)S(1)}, u32[]{:S(2)}, u32[]{:S(2)}) %all-to-all-start.1) | async-done | bytes 1048608 | tf_op jit(solution)/shard_map/all_to_all | solution.py:66
  37.9 78.5 %while.23 = (s32[]{:T(128)}, f32[16,512,128]{2,1,0:T(8,128)}, s32[4,1024]{1,0:T(4,128)S(1)}, s32[16]{0:T(128)S(1)}, bf16[4096,128]{1,0:T(8,128)(2,1)S(1)}, /*index=5*/s32[]{:T(128)}, s32[1]{0:T(128)}) while((s32[]{:T(128)}, f32[16,512,128]{2,1,0:T(8,128)}, s32[4,1024]{1,0:T(4,128)S(1)}, s32[16]{0:T(128)S(1)}, ...), condition=%wide.region_3.4_spmd.clone, body=%wide.region_2.3_spmd.clone.sunk | while | flops 538968576 | bytes 1364085 | solution.py:25
  39.2 3.7 fusion.30
  44.1 3.7 fusion.30
  49.0 3.7 fusion.30
  53.9 3.7 fusion.30
  58.8 3.7 fusion.30
  63.8 3.7 fusion.30
  68.7 3.7 fusion.30
  73.6 3.7 fusion.30
  78.5 3.7 fusion.30
  83.4 3.7 fusion.30
  88.3 3.7 fusion.30
  93.2 3.7 fusion.30
  98.1 3.7 fusion.30
  103.0 3.7 fusion.30
  107.9 3.7 fusion.30
  112.8 3.7 fusion.30
  116.5 2.0 collective-permute-start
  118.5 90.5 %collective-permute-done = f32[2,4096,128]{2,1,0:T(8,128)S(1)} collective-permute-done((f32[2,4096,128]{2,1,0:T(8,128)}, f32[2,4096,128]{2,1,0:T(8,128)S(1)}, u32[]{:S(2)}, u32[]{:S(2)}) %collective-permute-start) | collective-permute-done | bytes 4194336 | tf_op jit(solution)/shard_map/ppermute | solution.py:79
  208.9 2.7 bitcast_add_fusion
  213.5 89.6 %collective-permute-done.1 = f32[2,4096,128]{2,1,0:T(8,128)S(1)} collective-permute-done((f32[2,4096,128]{2,1,0:T(8,128)S(1)}, f32[2,4096,128]{2,1,0:T(8,128)S(1)}, u32[]{:S(2)}, u32[]{:S(2)}) %collective-permute-start.1) | collective-permute-done | bytes 4194336 | tf_op jit(solution)/shard_map/ppermute | solution.py:79
  303.5 2.7 collective-permute-start.2
  306.2 178.7 %collective-permute-done.2 = f32[2,4096,128]{2,1,0:T(8,128)S(1)} collective-permute-done((f32[2,4096,128]{2,1,0:T(8,128)S(1)}, f32[2,4096,128]{2,1,0:T(8,128)S(1)}, u32[]{:S(2)}, u32[]{:S(2)}) %collective-permute-start.2) | collective-permute-done | bytes 4194336 | tf_op jit(solution)/shard_map/ppermute | solution.py:79
  486.8 3.2 divide_subtract_fusion
  (67 shorter events, 15.8 us)
Async XLA Ops:
  2.0 18.0 %all-to-all-start = ((s32[4,1,1024]{2,1,0:T(1,128)}), s32[4,1,1024]{2,1,0:T(1,128)S(1)}, u32[]{:S(2)}, u32[]{:S(2)}) async-start(s32[4,1,1024]{2,1,0:T(1,128)} %compare_select_fusion), calls=%async_computation | async-start | bytes 32768 | tf_op jit(solution)/shard_map/all_to_all | solution.py:67
  20.0 17.9 %all-to-all-start.1 = ((bf16[4,1024,128]{2,1,0:T(8,128)(2,1)}), bf16[4,1024,128]{2,1,0:T(8,128)(2,1)S(1)}, u32[]{:S(2)}, u32[]{:S(2)}) async-start(bf16[4,1024,128]{2,1,0:T(8,128)(2,1)} %get-tuple-element.61), calls=%async_computation.1 | async-start | bytes 2097152 | tf_op jit(solution)/shard_map/all_to_all | solution.py:66
  116.5 92.5 %collective-permute-start = (f32[2,4096,128]{2,1,0:T(8,128)}, f32[2,4096,128]{2,1,0:T(8,128)S(1)}, u32[]{:S(2)}, u32[]{:S(2)}) collective-permute-start(f32[2,4096,128]{2,1,0:T(8,128)} %bitcast.43), channel_id=1, source_target_pairs={{0,4},{4,0},{8,12},{12,8},{16,20},{20,16},{24,28},{28,24},{1,5},{5... | collective-permute-start | bytes 12582920 | tf_op jit(solution)/shard_map/ppermute | solution.py:79
  211.7 91.5 %collective-permute-start.1 = (f32[2,4096,128]{2,1,0:T(8,128)S(1)}, f32[2,4096,128]{2,1,0:T(8,128)S(1)}, u32[]{:S(2)}, u32[]{:S(2)}) collective-permute-start(f32[2,4096,128]{2,1,0:T(8,128)S(1)} %bitcast_add_fusion), channel_id=1, source_target_pairs={{0,8},{4,12},{8,0},{12,4},{16,24},{20,28},{24,16},{28,20},{1,9},{5... | collective-permute-start | bytes 12582920 | tf_op jit(solution)/shard_map/ppermute | solution.py:79
  303.5 182.6 %copy-start.1 = (f32[2,4096]{1,0:T(2,128)S(1)}, f32[2,4096]{1,0:T(2,128)}, u32[]{:S(2)}) copy-start(f32[2,4096]{1,0:T(2,128)} %param.15) | copy-start | bytes 98308
  303.5 183.3 %copy-start = (f32[2,4096,128]{2,1,0:T(8,128)S(1)}, f32[2,4096,128]{2,1,0:T(8,128)}, u32[]{:S(2)}) copy-start(f32[2,4096,128]{2,1,0:T(8,128)} %param.14) | copy-start | bytes 12582916
  303.5 181.4 %collective-permute-start.2 = (f32[2,4096,128]{2,1,0:T(8,128)S(1)}, f32[2,4096,128]{2,1,0:T(8,128)S(1)}, u32[]{:S(2)}, u32[]{:S(2)}) collective-permute-start(f32[2,4096,128]{2,1,0:T(8,128)S(1)} %add.37), channel_id=1, source_target_pairs={{0,16},{4,20},{8,24},{12,28},{16,0},{20,4},{24,8},{28,12},{1,17},{... | collective-permute-start | bytes 12582920 | tf_op jit(solution)/shard_map/ppermute | solution.py:79
